TPU v7x, 32 devices: a whole 2x2x4 slice. The times are simulated.
32 devices in a mesh: dp: 16 (over z, y, core), shard: 2 (over x).
Axes of the slice: x: 2, y: 2, z: 4, core: 2. Of those that a mesh axis runs over, the one named last changes fastest.
Arguments:
- tokens: float32 [16384, 1024], P(('dp', 'shard')), may hold values from -6 to 6
- out_grad: float32 [16384, 1024], P(('dp', 'shard')), may hold values from -30 to 30
- segment_ids: int32 [16, 1024], P('dp'), may hold values from 0 to 3, never falling along the last dimension, each value on 1 to 512 neighbouring positions
- qkv_weight: float32 [1024, 3072], P('dp', 'shard'), may hold values from -0.1875 to 0.1875
- proj_weight: float32 [1024, 1024], P('dp', 'shard'), may hold values from -1.5 to 1.5
- up_weight: float32 [1024, 4096], P('dp', 'shard'), may hold values from -0.1875 to 0.1875
- down_weight: float32 [4096, 1024], P('dp', 'shard'), may hold values from -0.09375 to 0.09375
- vectors: float32 [12, 1024], P(None, ('dp', 'shard')), may hold values from -4 to 4
- qkv_moments: float32 [2, 1024, 3072], P(None, 'dp', 'shard'), may hold values from -0.05 to 0.05
- proj_moments: float32 [2, 1024, 1024], P(None, 'dp', 'shard'), may hold values from -0.05 to 0.05
- up_moments: float32 [2, 1024, 4096], P(None, 'dp', 'shard'), may hold values from -0.05 to 0.05
- down_moments: float32 [2, 4096, 1024], P(None, 'dp', 'shard'), may hold values from -0.05 to 0.05
- vector_moments: float32 [2, 12, 1024], P(None, None, ('dp', 'shard')), may hold values from -1 to 1
Outputs:
- block_out: float32 [16384, 1024], P(('dp', 'shard'))
- tokens_grad: float32 [16384, 1024], P(('dp', 'shard'))
- qkv_grad: float32 [1024, 3072], P('dp', 'shard')
- proj_grad: float32 [1024, 1024], P('dp', 'shard')
- up_grad: float32 [1024, 4096], P('dp', 'shard')
- down_grad: float32 [4096, 1024], P('dp', 'shard')
- vectors_grad: float32 [12, 1024], P(None, ('dp', 'shard'))
- qkv_new: float32 [1024, 3072], P('dp', 'shard')
- proj_new: float32 [1024, 1024], P('dp', 'shard')
- up_new: float32 [1024, 4096], P('dp', 'shard')
- down_new: float32 [4096, 1024], P('dp', 'shard')
- vectors_new: float32 [12, 1024], P(None, ('dp', 'shard'))
- qkv_moments_new: float32 [2, 1024, 3072], P(None, 'dp', 'shard')
- proj_moments_new: float32 [2, 1024, 1024], P(None, 'dp', 'shard')
- up_moments_new: float32 [2, 1024, 4096], P(None, 'dp', 'shard')
- down_moments_new: float32 [2, 4096, 1024], P(None, 'dp', 'shard')
- vector_moments_new: float32 [2, 12, 1024], P(None, None, ('dp', 'shard'))
All inputs are finite; a program needn't handle non-finite values.
Results may differ from a plain program's by a relative error of at most 0.011.
Values may be sent and summed in bfloat16 or wider, within the bound.
A program may use at most 320 MiB of HBM per device.

v0:
```python
import math
import jax
import jax.numpy as jnp
from jax import lax
from jax.sharding import PartitionSpec as P

D = 1024
FF = 4096
HD = 64
ROT = 16
STEP = 4
VROWS = 12
NPARAM = 12595200
ln_eps = 1e-05
beta_one = 0.9
beta_two = 0.95
learn_rate = 0.005
decay_rate = 0.01
adam_eps = 1e-08
rope_base = 10000.0


def norm_rows(inputs, gain_row, bias_row):
    center = inputs - jnp.mean(inputs, axis=-1, keepdims=True)
    inverse = lax.rsqrt(jnp.mean(center * center, axis=-1, keepdims=True) + ln_eps)
    unit_rows = center * inverse
    return (unit_rows * gain_row + bias_row, unit_rows, inverse)


def norm_back(upstream, unit_rows, inverse, gain_row):
    gain_grad = jnp.sum(upstream * unit_rows, axis=0)
    bias_grad = jnp.sum(upstream, axis=0)
    scaled_up = upstream * gain_row
    mean_plain = jnp.mean(scaled_up, axis=-1, keepdims=True)
    mean_unit = jnp.mean(scaled_up * unit_rows, axis=-1, keepdims=True)
    return (inverse * (scaled_up - mean_plain - unit_rows * mean_unit), gain_grad, bias_grad)


def doc_positions(segment_row):
    length_all = segment_row.shape[0]
    indices = jnp.arange(length_all, dtype=jnp.int32)
    starting = jnp.concatenate(
        [jnp.ones((1,), dtype=jnp.bool_), segment_row[1:] != segment_row[:-1]]
    )
    begins = lax.cummax(jnp.where(starting, indices, 0), axis=0)
    return indices - begins


def rotary_tables(positions, rot_dims):
    half_dims = rot_dims // 2
    exponent = jnp.arange(half_dims, dtype=jnp.float32) * (2.0 / rot_dims)
    inverse_freq = jnp.exp(-math.log(rope_base) * exponent)
    angles = positions.astype(jnp.float32)[:, None] * inverse_freq[None, :]
    return (jnp.cos(angles)[:, None, :], jnp.sin(angles)[:, None, :])


def rotate(head_rows, cosine_table, sine_table):
    half_dims = cosine_table.shape[-1]
    lower_half = head_rows[..., :half_dims]
    upper_half = head_rows[..., half_dims : 2 * half_dims]
    return jnp.concatenate(
        [
            lower_half * cosine_table - upper_half * sine_table,
            upper_half * cosine_table + lower_half * sine_table,
            head_rows[..., 2 * half_dims :],
        ],
        axis=-1,
    )


def gelu_pair(pre_act):
    normal_cdf = 0.5 * (1.0 + lax.erf(pre_act * (1.0 / math.sqrt(2.0))))
    density = jnp.exp(-0.5 * pre_act * pre_act) * (1.0 / math.sqrt(2.0 * math.pi))
    return (pre_act * normal_cdf, normal_cdf + pre_act * density)


def times_transposed(left, right):
    return lax.dot_general(
        left, right, (((1,), (1,)), ((), ())), preferred_element_type=jnp.float32
    )


def transposed_times(left, right):
    return lax.dot_general(
        left, right, (((0,), (0,)), ((), ())), preferred_element_type=jnp.float32
    )


def adam_update(weight, moments, gradient, clip_factor):
    clipped = gradient * clip_factor
    first_new = beta_one * moments[0] + (1.0 - beta_one) * clipped
    second_new = beta_two * moments[1] + (1.0 - beta_two) * clipped * clipped
    fix_first = 1.0 - math.pow(beta_one, STEP)
    fix_second = 1.0 - math.pow(beta_two, STEP)
    direction = first_new / fix_first / (jnp.sqrt(second_new / fix_second) + adam_eps)
    return (
        weight - learn_rate * (direction + decay_rate * weight),
        jnp.stack([first_new, second_new]),
    )


def shards(
    tokens,
    out_grad,
    segment_ids,
    qkv_weight,
    proj_weight,
    up_weight,
    down_weight,
    vectors,
    qkv_moments,
    proj_moments,
    up_moments,
    down_moments,
    vector_moments,
):
    columns_full = (
        lax.all_gather(qkv_weight.astype(jnp.bfloat16), "shard", axis=1, tiled=True),
        lax.all_gather(proj_weight.astype(jnp.bfloat16), "shard", axis=1, tiled=True),
        lax.all_gather(up_weight.astype(jnp.bfloat16), "shard", axis=1, tiled=True),
        lax.all_gather(down_weight.astype(jnp.bfloat16), "shard", axis=1, tiled=True),
        lax.all_gather(vectors.astype(jnp.bfloat16), "shard", axis=1, tiled=True),
    )
    qkv_work, proj_work, up_work, down_work, vec_bf = (
        lax.all_gather(columns_full[0], "dp", axis=0, tiled=True),
        lax.all_gather(columns_full[1], "dp", axis=0, tiled=True),
        lax.all_gather(columns_full[2], "dp", axis=0, tiled=True),
        lax.all_gather(columns_full[3], "dp", axis=0, tiled=True),
        lax.all_gather(columns_full[4], "dp", axis=1, tiled=True),
    )
    vec_work = vec_bf.astype(jnp.float32)
    head_count = D // HD
    score_scale = 1.0 / math.sqrt(HD)
    local_rows = tokens.shape[0]
    segment_row = segment_ids[0]
    length_all = segment_row.shape[0]
    row_start = lax.axis_index("shard") * local_rows
    query_index = row_start + jnp.arange(local_rows, dtype=jnp.int32)
    query_segment = lax.dynamic_slice_in_dim(segment_row, row_start, local_rows)
    positions = lax.dynamic_slice_in_dim(doc_positions(segment_row), row_start, local_rows)
    normed_one, unit_one, inverse_one = norm_rows(tokens, vec_work[0], vec_work[1])
    hidden_one = normed_one.astype(jnp.bfloat16)
    mixed_rows = jnp.dot(hidden_one, qkv_work, preferred_element_type=jnp.float32)
    query_raw = (mixed_rows[:, :D] + vec_work[4]).reshape(local_rows, head_count, HD)
    key_raw = mixed_rows[:, D : 2 * D].reshape(local_rows, head_count, HD)
    value_bf = (mixed_rows[:, 2 * D :] + vec_work[5]).astype(jnp.bfloat16)
    cosine_table, sine_table = rotary_tables(positions, ROT)
    query_bf = rotate(query_raw, cosine_table, sine_table).astype(jnp.bfloat16)
    key_bf = rotate(key_raw, cosine_table, sine_table).astype(jnp.bfloat16).reshape(local_rows, D)
    key_piece = lax.all_gather(key_bf, "shard", axis=0, tiled=True)
    value_piece = lax.all_gather(value_bf, "shard", axis=0, tiled=True)
    piece_rows = key_piece.shape[0]
    key_heads = key_piece.reshape(piece_rows, head_count, HD)
    value_heads = value_piece.reshape(piece_rows, head_count, HD)
    key_index = jnp.arange(piece_rows, dtype=jnp.int32)
    allowed = (segment_row[None, :] == query_segment[:, None]) & (
        key_index[None, :] <= query_index[:, None]
    )
    scores = (
        jnp.einsum("qhd,khd->hqk", query_bf, key_heads, preferred_element_type=jnp.float32)
        * score_scale
    )
    exp_scores = jnp.where(allowed[None], jnp.exp(scores), 0.0)
    numerator = jnp.einsum(
        "hqk,khd->qhd",
        exp_scores.astype(jnp.bfloat16),
        value_heads,
        preferred_element_type=jnp.float32,
    )
    numerator, totals = (numerator, jnp.sum(exp_scores, axis=-1))
    attended = numerator / jnp.transpose(totals)[:, :, None]
    log_totals = jnp.log(totals)
    attended_bf = attended.reshape(local_rows, D).astype(jnp.bfloat16)
    proj_out = jnp.dot(attended_bf, proj_work, preferred_element_type=jnp.float32) + vec_work[6]
    normed_two, unit_two, inverse_two = norm_rows(tokens, vec_work[2], vec_work[3])
    hidden_two = normed_two.astype(jnp.bfloat16)
    pre_act = jnp.dot(hidden_two, up_work, preferred_element_type=jnp.float32) + vec_work[
        8:
    ].reshape(FF)
    act_values, act_slope = gelu_pair(pre_act)
    act_bf = act_values.astype(jnp.bfloat16)
    block_out = (
        tokens
        + proj_out
        + (jnp.dot(act_bf, down_work, preferred_element_type=jnp.float32) + vec_work[7])
    )
    cot_bf = out_grad.astype(jnp.bfloat16)
    down_part = transposed_times(act_bf, cot_bf)
    proj_part = transposed_times(attended_bf, cot_bf)
    cot_sum = jnp.sum(out_grad, axis=0)
    grad_pre = times_transposed(cot_bf, down_work) * act_slope
    grad_pre_bf = grad_pre.astype(jnp.bfloat16)
    up_part = transposed_times(hidden_two, grad_pre_bf)
    rows_two, ln2_gain_part, ln2_bias_part = norm_back(
        times_transposed(grad_pre_bf, up_work), unit_two, inverse_two, vec_work[2]
    )
    grad_att_bf = (
        times_transposed(cot_bf, proj_work).astype(jnp.bfloat16).reshape(local_rows, head_count, HD)
    )
    keys_all, values_all = (
        lax.all_gather(key_bf, "shard", axis=0, tiled=True),
        lax.all_gather(value_bf, "shard", axis=0, tiled=True),
    )
    key_heads = keys_all.reshape(length_all, head_count, HD)
    value_heads = values_all.reshape(length_all, head_count, HD)
    key_index = jnp.arange(length_all, dtype=jnp.int32)
    allowed = (segment_row[None, :] == query_segment[:, None]) & (
        key_index[None, :] <= query_index[:, None]
    )
    scores = (
        jnp.einsum("qhd,khd->hqk", query_bf, key_heads, preferred_element_type=jnp.float32)
        * score_scale
    )
    probability = jnp.where(allowed[None], jnp.exp(scores - log_totals[:, :, None]), 0.0)
    grad_prob = jnp.einsum(
        "qhd,khd->hqk", grad_att_bf, value_heads, preferred_element_type=jnp.float32
    )
    row_delta = jnp.transpose(jnp.sum(grad_att_bf.astype(jnp.float32) * attended, axis=-1))
    grad_score = (probability * (grad_prob - row_delta[:, :, None]) * score_scale).astype(
        jnp.bfloat16
    )
    grad_query = jnp.einsum(
        "hqk,khd->qhd", grad_score, key_heads, preferred_element_type=jnp.float32
    )
    grad_query = rotate(grad_query, cosine_table, -sine_table).reshape(local_rows, D)
    key_terms = jnp.einsum(
        "hqk,qhd->khd", grad_score, query_bf, preferred_element_type=jnp.float32
    ).reshape(length_all, D)
    value_terms = jnp.einsum(
        "hqk,qhd->khd",
        probability.astype(jnp.bfloat16),
        grad_att_bf,
        preferred_element_type=jnp.float32,
    ).reshape(length_all, D)
    key_value_grad = lax.psum_scatter(
        jnp.concatenate([key_terms, value_terms], axis=1), "shard", scatter_dimension=0, tiled=True
    )
    grad_key = rotate(
        key_value_grad[:, :D].reshape(local_rows, head_count, HD), cosine_table, -sine_table
    ).reshape(local_rows, D)
    grad_value = key_value_grad[:, D:]
    grad_mixed_bf = jnp.concatenate([grad_query, grad_key, grad_value], axis=1).astype(jnp.bfloat16)
    qkv_part = transposed_times(hidden_one, grad_mixed_bf)
    rows_one, ln1_gain_part, ln1_bias_part = norm_back(
        times_transposed(grad_mixed_bf, qkv_work), unit_one, inverse_one, vec_work[0]
    )
    tokens_grad = out_grad + rows_one + rows_two
    vec_part = jnp.concatenate(
        [
            jnp.stack(
                [
                    ln1_gain_part,
                    ln1_bias_part,
                    ln2_gain_part,
                    ln2_bias_part,
                    jnp.sum(grad_query, axis=0),
                    jnp.sum(grad_value, axis=0),
                    cot_sum,
                    cot_sum,
                ]
            ),
            jnp.sum(grad_pre, axis=0).reshape(FF // D, D),
        ],
        axis=0,
    )
    groups = lax.axis_size("dp")
    members = lax.axis_size("shard")
    owners = groups * members
    vec_split = vec_part.reshape(VROWS, groups, members, D // owners)
    group_sums = (
        lax.psum_scatter(qkv_part, "shard", scatter_dimension=1, tiled=True),
        lax.psum_scatter(proj_part, "shard", scatter_dimension=1, tiled=True),
        lax.psum_scatter(up_part, "shard", scatter_dimension=1, tiled=True),
        lax.psum_scatter(down_part, "shard", scatter_dimension=1, tiled=True),
        lax.psum_scatter(vec_split, "shard", scatter_dimension=2, tiled=True),
    )
    owner_sums = (
        lax.psum_scatter(group_sums[0], "dp", scatter_dimension=0, tiled=True),
        lax.psum_scatter(group_sums[1], "dp", scatter_dimension=0, tiled=True),
        lax.psum_scatter(group_sums[2], "dp", scatter_dimension=0, tiled=True),
        lax.psum_scatter(group_sums[3], "dp", scatter_dimension=0, tiled=True),
        lax.psum_scatter(group_sums[4], "dp", scatter_dimension=1, tiled=True),
    )
    qkv_grad = owner_sums[0]
    proj_grad = owner_sums[1]
    up_grad = owner_sums[2]
    down_grad = owner_sums[3]
    vectors_grad = owner_sums[4].reshape(VROWS, D // owners)
    local_square = (
        jnp.sum(qkv_grad * qkv_grad)
        + jnp.sum(proj_grad * proj_grad)
        + jnp.sum(up_grad * up_grad)
        + jnp.sum(down_grad * down_grad)
        + jnp.sum(vectors_grad * vectors_grad)
    )
    square_total = lax.psum(local_square, ("dp", "shard"))
    norm_limit = math.sqrt(NPARAM)
    clip_factor = norm_limit / jnp.maximum(jnp.sqrt(square_total), norm_limit)
    qkv_new, qkv_moments_new = adam_update(qkv_weight, qkv_moments, qkv_grad, clip_factor)
    proj_new, proj_moments_new = adam_update(proj_weight, proj_moments, proj_grad, clip_factor)
    up_new, up_moments_new = adam_update(up_weight, up_moments, up_grad, clip_factor)
    down_new, down_moments_new = adam_update(down_weight, down_moments, down_grad, clip_factor)
    vectors_new, vector_moments_new = adam_update(
        vectors, vector_moments, vectors_grad, clip_factor
    )
    return (
        block_out,
        tokens_grad,
        qkv_grad,
        proj_grad,
        up_grad,
        down_grad,
        vectors_grad,
        qkv_new,
        proj_new,
        up_new,
        down_new,
        vectors_new,
        qkv_moments_new,
        proj_moments_new,
        up_moments_new,
        down_moments_new,
        vector_moments_new,
    )


def solution(mesh):
    placed = (
        P(("dp", "shard"), None),
        P(("dp", "shard"), None),
        P("dp", None),
        P("dp", "shard"),
        P("dp", "shard"),
        P("dp", "shard"),
        P("dp", "shard"),
        P(None, ("dp", "shard")),
        P(None, "dp", "shard"),
        P(None, "dp", "shard"),
        P(None, "dp", "shard"),
        P(None, "dp", "shard"),
        P(None, None, ("dp", "shard")),
    )
    return jax.shard_map(
        shards,
        mesh=mesh,
        in_specs=placed,
        out_specs=(
            P(("dp", "shard"), None),
            P(("dp", "shard"), None),
            P("dp", "shard"),
            P("dp", "shard"),
            P("dp", "shard"),
            P("dp", "shard"),
            P(None, ("dp", "shard")),
            P("dp", "shard"),
            P("dp", "shard"),
            P("dp", "shard"),
            P("dp", "shard"),
            P(None, ("dp", "shard")),
            P(None, "dp", "shard"),
            P(None, "dp", "shard"),
            P(None, "dp", "shard"),
            P(None, "dp", "shard"),
            P(None, None, ("dp", "shard")),
        ),
        check_vma=False,
    )
```

profile of v0, /device:TPU:0, one launch (start us, length us, event | category | flops | bytes accessed | tf_op | source)
XLA Modules:
  0.0 1481.1 jit_solution(18126317219042445174)
XLA Ops:
  7.3 1.2 convert_element_type.70
  8.4 8.6 all_gather.40
  18.1 5.0 all_gather.44
  23.2 4.4 all-gather
  27.7 22.3 %all-gather.1 = bf16[16,64,12]{1,2,0:T(8,128)(2,1)S(1)} all-gather(bf16[1,64,12]{1,2,0:T(8,128)(2,1)S(1)} %reshape.337), channel_id=1, replica_groups=mesh['dp'=16,'shard'=2] {'dp'}, dimensions={0}, use_global_device_ids=true | all-gather | bytes 26112 | tf_op jit(solution)/shard_map/all_gather | solution.py:129
  52.8 27.5 %all-gather.9.cloned.1.call-done = bf16[1024,3072]{1,0:T(8,128)(2,1)} async-done(((bf16[64,3072]{1,0:T(8,128)(2,1)}), bf16[1024,3072]{1,0:T(8,128)(2,1)}) %all-gather.9.cloned.1.call-update) | async-done | bytes 6291472 | tf_op jit(solution)/shard_map/all_gather | solution.py:125
  80.3 5.8 fusion.31
  86.1 2.3 slice_add_fusion
  88.4 2.9 copy.69
  91.3 1.8 copy.70
  93.1 1.5 slice.266
  94.6 2.0 subtract_convert_fusion.2
  98.4 9.4 all_gather.46
  107.9 8.4 all_gather.48
  116.4 1.4 fusion.19
  118.6 4.1 all-gather.15.cloned.1.call-done
  122.7 2.9 convolution_convert_fusion
  125.6 1.5 copy.71
  127.1 1.5 slice.267
  128.6 28.0 %all-gather.13.cloned.1.call-done = bf16[1024,1024]{0,1:T(8,128)(2,1)} async-done(((bf16[512,1024]{0,1:T(8,128)(2,1)}), bf16[1024,1024]{0,1:T(8,128)(2,1)}) %all-gather.13.cloned.1.call-update) | async-done | bytes 2097168 | tf_op jit(solution)/shard_map/all_gather | solution.py:150
  156.6 17.5 %fusion = (f32[16,512]{1,0:T(8,128)S(1)}, f32[16,512,1024]{2,1,0:T(8,128)}) fusion(pred[512,1024]{1,0:T(8,128)(4,1)S(1)} %copy-done.22, bf16[1024,16,64]{0,2,1:T(8,128)(2,1)} %bitcast.176, bf16[512,16,48]{0,2,1:T(8,128)(2,1)S(1)} %slice.267, bf16[512,16,8]{0,2,1:T(8,128)(2,1)S(1)} %copy-done.23, bf16[512,16,8]{0,2,1:T(8,128)(2,1)S(1)} %get-tuple-element.73), kind=kOutput, calls=%fused_computation.3 | convolution fusion | flops 1102045184 | bytes 37257216 | tf_op jit(solution)/shard_map/qhd,khd->hqk/dot_general | solution.py:160
  174.2 17.6 %all-gather.11.cloned.1.call-done = bf16[1024,1024]{1,0:T(8,128)(2,1)} async-done(((bf16[512,1024]{1,0:T(8,128)(2,1)}), bf16[1024,1024]{1,0:T(8,128)(2,1)}) %all-gather.11.cloned.1.call-update) | async-done | bytes 2097168 | tf_op jit(solution)/shard_map/all_gather | solution.py:151
  191.7 2.9 copy.68
  194.6 15.7 %multiply_reduce_fusion.4 = (f32[512,16]{0,1:T(8,128)S(1)}, bf16[512,16,64]{0,2,1:T(8,128)(2,1)}) fusion(bf16[512,1024]{0,1:T(8,128)(2,1)} %copy.71, f32[512,16]{0,1:T(8,128)S(1)} %bitcast.190, bf16[1024,16,64]{0,2,1:T(8,128)(2,1)S(1)} %bitcast.178, f32[16,512,1024]{2,1,0:T(8,128)} %get-tuple-element.113, pred[512,1024]{1,0:T(8,128)(4,1)} %fusion.19), kind=kOutput, calls=%fused_computation.34 | convolution fusion | flops 1101520896 | bytes 38338560 | tf_op jit(solution)/shard_map/hqk,khd->qhd/dot_general | solution.py:164
  210.3 22.3 %multiply_convert_fusion = bf16[16,512,1024]{2,1,0:T(8,128)(2,1)} fusion(f32[16,512,1024]{2,1,0:T(8,128)} %get-tuple-element.113, f32[16,512]{1,0:T(8,128)S(1)} %bitcast.212, f32[16,512]{1,0:T(8,128)S(1)} %log.7, pred[512,1024]{1,0:T(8,128)(4,1)} %fusion.19, bf16[512,16,64]{0,2,1:T(8,128)(2,1)} %bitcast.184, bf16[1024,16,64]{0,2,1:T(8,128)(2,1)S(1)} %bitcast.179), kind=kOutput, calls=%fused_computation | convolution fusion | flops 1132462080 | bytes 54067200 | tf_op jit(solution)/shard_map/qhd,khd->hqk/dot_general | solution.py:215
  232.7 9.0 fusion.28
  241.7 16.6 %fusion.5 = f32[16,64,1024]{2,1,0:T(8,128)} fusion(bf16[512,16,64]{0,2,1:T(8,128)(2,1)} %bitcast.185, f32[16,512,1024]{2,1,0:T(8,128)} %get-tuple-element.113, f32[16,512]{1,0:T(8,128)} %copy-done.31, pred[512,1024]{1,0:T(8,128)(4,1)} %fusion.19), kind=kOutput, calls=%fused_computation.7 | convolution fusion | flops 1107296256 | bytes 39354368 | tf_op jit(solution)/shard_map/hqk,qhd->khd/dot_general | solution.py:229
  258.3 6.8 pad_maximum_fusion
  266.8 3.2 fusion.70
  271.6 10.7 multiply_convert_fusion.1
  282.3 60.7 %all-gather.19.cloned.1.call-done = bf16[4096,1024]{1,0:T(8,128)(2,1)} async-done(((bf16[256,1024]{1,0:T(8,128)(2,1)}), bf16[4096,1024]{1,0:T(8,128)(2,1)}) %all-gather.19.cloned.1.call-update) | async-done | bytes 8388624 | tf_op jit(solution)/shard_map/all_gather | solution.py:128
  343.0 10.7 fusion.68
  353.7 2.0 copy-done.47
  355.7 8.4 fusion.15
  364.1 10.6 fusion.71
  375.0 13.2 convolution_bitcast_fusion
  388.2 2.7 slice.189
  390.9 52.3 %reduce-scatter.12.cloned.1.call-done = f32[512,2048]{0,1:T(8,128)} async-done(((f32[1024,2048]{0,1:T(8,128)}), f32[512,2048]{0,1:T(8,128)}) %reduce-scatter.12.cloned.1.call-update) | async-done | bytes 4194320 | tf_op jit(solution)/shard_map/reduce_scatter | solution.py:235
  443.2 2.5 slice_reduce_fusion
  445.9 1.8 slice.264
  447.8 1.5 multiply_subtract_fusion.3
  450.9 9.6 fusion.24
  461.4 38.5 %reduce-scatter.18.cloned.1.call-done = f32[1024,512]{1,0:T(8,128)} async-done(((f32[1024,1024]{1,0:T(8,128)}), f32[1024,512]{1,0:T(8,128)}) %reduce-scatter.18.cloned.1.call-update) | async-done | bytes 2097168 | tf_op jit(solution)/shard_map/reduce_scatter | solution.py:272
  500.2 8.6 fusion.25
  509.2 11.7 multiply_reduce_fusion
  522.2 169.3 %reduce-scatter.22.cloned.1.call-done = f32[1024,2048]{1,0:T(8,128)} async-done(((f32[1024,4096]{1,0:T(8,128)}), f32[1024,2048]{1,0:T(8,128)}) %reduce-scatter.22.cloned.1.call-update) | async-done | bytes 8388624 | tf_op jit(solution)/shard_map/reduce_scatter | solution.py:273
  691.6 191.3 %reduce-scatter.26.cloned.1.call-done = f32[4096,512]{1,0:T(8,128)} async-done(((f32[4096,1024]{1,0:T(8,128)}), f32[4096,512]{1,0:T(8,128)}) %reduce-scatter.26.cloned.1.call-update) | async-done | bytes 8388624 | tf_op jit(solution)/shard_map/reduce_scatter | solution.py:274
  883.0 146.8 %reduce-scatter.14.cloned.1.call-done = f32[1024,1536]{1,0:T(8,128)} async-done(((f32[1024,3072]{1,0:T(8,128)}), f32[1024,1536]{1,0:T(8,128)}) %reduce-scatter.14.cloned.1.call-update) | async-done | bytes 6291472 | tf_op jit(solution)/shard_map/reduce_scatter | solution.py:271
  1031.1 8.3 fusion.69
  1039.4 2.6 add_add_fusion
  1042.0 53.7 %reduce-scatter.20.cloned.1.call-done = f32[64,512]{1,0:T(8,128)} async-done(((f32[1024,512]{1,0:T(8,128)}), f32[64,512]{1,0:T(8,128)}) %reduce-scatter.20.cloned.1.call-update) | async-done | bytes 131088 | tf_op jit(solution)/shard_map/reduce_scatter | solution.py:279
  1095.8 1.5 multiply_reduce_fusion.11
  1097.3 11.3 reduce-scatter.30.cloned.1.call-done
  1108.6 65.1 %all-reduce = f32[12,16,1,32]{3,2,1,0:T(1,128)S(1)} all-reduce(f32[12,16,1,32]{3,2,1,0:T(1,128)} %bitcast.188), channel_id=12, replica_groups=mesh['dp'=16,'shard'=2] {'dp'}, use_global_device_ids=true, to_apply=%region_28.29.clone | all-reduce | flops 6144 | bytes 49152
  1175.0 42.1 %reduce-scatter.24.cloned.1.call-done = f32[64,2048]{1,0:T(8,128)} async-done(((f32[1024,2048]{1,0:T(8,128)}), f32[64,2048]{1,0:T(8,128)}) %reduce-scatter.24.cloned.1.call-update) | async-done | bytes 524304 | tf_op jit(solution)/shard_map/reduce_scatter | solution.py:280
  1217.1 1.8 multiply_reduce_fusion.9
  1218.9 105.8 %reduce-scatter.28.cloned.1.call-done = f32[256,512]{1,0:T(8,128)} async-done(((f32[4096,512]{1,0:T(8,128)}), f32[256,512]{1,0:T(8,128)}) %reduce-scatter.28.cloned.1.call-update) | async-done | bytes 524304 | tf_op jit(solution)/shard_map/reduce_scatter | solution.py:281
  1324.7 1.8 multiply_reduce_fusion.8
  1326.5 87.3 %reduce-scatter.16.cloned.1.call-done = f32[64,1536]{1,0:T(8,128)} async-done(((f32[1024,1536]{1,0:T(8,128)}), f32[64,1536]{1,0:T(8,128)}) %reduce-scatter.16.cloned.1.call-update) | async-done | bytes 393232 | tf_op jit(solution)/shard_map/reduce_scatter | solution.py:278
  1413.8 1.7 multiply_reduce_fusion.10
  1418.8 4.4 multiply_add_fusion
  1423.2 39.6 %psum.7 = f32[]{:T(128)} all-reduce(f32[]{:T(128)S(6)} %add.283), channel_id=1, replica_groups=mesh['dp'=16,'shard'=2] {'dp','shard'}, use_global_device_ids=true, to_apply=%region_34.35 | all-reduce | flops 1 | bytes 8 | tf_op jit(solution)/shard_map/psum | solution.py:296
  1464.8 2.6 fusion.35
  1468.5 1.2 fusion.34
  (197 shorter events, 24.2 us)
Async XLA Ops:
  7.2 16.0 %copy-start.32 = (f32[12,32]{1,0:T(8,128)S(1)}, f32[12,32]{1,0:T(8,128)}, u32[]{:S(2)}) copy-start(f32[12,32]{1,0:T(8,128)} %param.20) | copy-start | bytes 4612
  7.2 42.8 %copy-start.30 = (s32[1,1024]{1,0:T(1,128)S(1)}, s32[1,1024]{1,0:T(1,128)}, u32[]{:S(2)}) copy-start(s32[1,1024]{1,0:T(1,128)} %param.15) | copy-start | bytes 12292
  7.2 43.4 %copy-start = (f32[512,1024]{1,0:T(8,128)S(1)}, f32[512,1024]{1,0:T(8,128)}, u32[]{:S(2)}) copy-start(f32[512,1024]{1,0:T(8,128)} %param.13) | copy-start | bytes 6291460
  7.2 73.1 %all-gather.9.cloned.1.call-start = ((), (), s32[]{:S(2)}) async-start(), calls=%async_computation.10 | async-start | bytes 6684672 | tf_op jit(solution)/shard_map/all_gather | solution.py:125
  17.1 105.6 %all-gather.15.cloned.1.call-start = ((), (), s32[]{:S(2)}) async-start(), calls=%async_computation.13 | async-start | bytes 2228224 | tf_op jit(solution)/shard_map/all_gather | solution.py:126
  23.1 133.5 %all-gather.13.cloned.1.call-start = ((), (), s32[]{:S(2)}) async-start(), calls=%async_computation.12 | async-start | bytes 3145728 | tf_op jit(solution)/shard_map/all_gather | solution.py:150
  50.0 2.2 copy-start.26
  52.2 42.4 %copy-start.27 = (f32[512,8]{0,1:T(8,128)}, f32[512,8]{0,1:T(8,128)S(1)}, u32[]{:S(2)}) copy-start(f32[512,8]{0,1:T(8,128)S(1)} %get-tuple-element.111) | copy-start | bytes 49156
  52.8 33.2 %copy-start.35 = (f32[1,1024]{1,0:T(1,128)}, f32[1,1024]{1,0:T(1,128)S(1)}, u32[]{:S(2)}) copy-start(f32[1,1024]{1,0:T(1,128)S(1)} %get-tuple-element.100) | copy-start | bytes 12292
  52.8 33.3 %copy-start.41 = (f32[1,1024]{1,0:T(1,128)}, f32[1,1024]{1,0:T(1,128)S(1)}, u32[]{:S(2)}) copy-start(f32[1,1024]{1,0:T(1,128)S(1)} %get-tuple-element.99) | copy-start | bytes 12292
  96.6 1.7 copy-start.7
  97.7 10.2 copy-start.5
  97.7 94.0 %all-gather.11.cloned.1.call-start = ((), (), s32[]{:S(2)}) async-start(), calls=%async_computation.11 | async-start | bytes 3145728 | tf_op jit(solution)/shard_map/all_gather | solution.py:151
  98.3 172.7 %all-gather.17.cloned.1.call-start = ((), (), s32[]{:S(2)}) async-start(), calls=%async_computation.14 | async-start | bytes 8912896 | tf_op jit(solution)/shard_map/all_gather | solution.py:127
  98.4 19.4 %copy-start.4 = (f32[512,1024]{1,0:T(8,128)S(1)}, f32[512,1024]{1,0:T(8,128)}, u32[]{:S(2)}) copy-start(f32[512,1024]{1,0:T(8,128)} %param.14) | copy-start | bytes 6291460
  107.8 235.2 %all-gather.19.cloned.1.call-start = ((), (), s32[]{:S(2)}) async-start(), calls=%async_computation.15 | async-start | bytes 8912896 | tf_op jit(solution)/shard_map/all_gather | solution.py:128
  116.3 326.9 %reduce-scatter.12.cloned.1.call-start = ((), (), s32[]{:S(2)}) async-start(), calls=%async_computation.16 | async-start | bytes 12582912 | tf_op jit(solution)/shard_map/reduce_scatter | solution.py:235
  118.6 7.0 copy-start.15
  125.6 31.1 %copy-start.22 = (pred[512,1024]{1,0:T(8,128)(4,1)S(1)}, pred[512,1024]{1,0:T(8,128)(4,1)}, u32[]{:S(2)}) copy-start(pred[512,1024]{1,0:T(8,128)(4,1)} %fusion.19) | copy-start | bytes 1572868
  125.6 31.1 %copy-start.23 = (bf16[512,16,8]{0,2,1:T(8,128)(2,1)S(1)}, bf16[512,16,8]{0,2,1:T(8,128)(2,1)}, u32[]{:S(2)}) copy-start(bf16[512,16,8]{0,2,1:T(8,128)(2,1)} %get-tuple-element.74) | copy-start | bytes 393220
  174.2 36.2 %copy-start.31 = (f32[16,512]{1,0:T(8,128)}, f32[16,512]{1,0:T(8,128)S(1)}, u32[]{:S(2)}) copy-start(f32[16,512]{1,0:T(8,128)S(1)} %log.7) | copy-start | bytes 98308
  210.3 22.3 %copy-start.24 = (bf16[512,16,8]{0,2,1:T(8,128)(2,1)S(1)}, bf16[512,16,8]{0,2,1:T(8,128)(2,1)}, u32[]{:S(2)}) copy-start(bf16[512,16,8]{0,2,1:T(8,128)(2,1)} %get-tuple-element.74) | copy-start | bytes 393220
  265.1 1.2 copy-start.16
  265.1 1.7 copy-start.44
  265.1 234.8 %reduce-scatter.18.cloned.1.call-start = ((), (), s32[]{:S(2)}) async-start(), calls=%async_computation.19 | async-start | bytes 6291456 | tf_op jit(solution)/shard_map/reduce_scatter | solution.py:272
  270.0 1.6 copy-start.1
  270.0 421.5 %reduce-scatter.22.cloned.1.call-start = ((), (), s32[]{:S(2)}) async-start(), calls=%async_computation.21 | async-start | bytes 25165824 | tf_op jit(solution)/shard_map/reduce_scatter | solution.py:273
  353.7 2.0 copy-start.47
  364.1 518.8 %reduce-scatter.26.cloned.1.call-start = ((), (), s32[]{:S(2)}) async-start(), calls=%async_computation.23 | async-start | bytes 25165824 | tf_op jit(solution)/shard_map/reduce_scatter | solution.py:274
  374.8 655.0 %reduce-scatter.14.cloned.1.call-start = ((), (), s32[]{:S(2)}) async-start(), calls=%async_computation.17 | async-start | bytes 18874368 | tf_op jit(solution)/shard_map/reduce_scatter | solution.py:271
  445.8 2.0 copy-start.28
  445.8 2.0 copy-start.29
  445.9 3.4 copy-start.2
  447.8 1.9 copy-start.17
  449.4 1.6 copy-start.36
  449.4 1.6 copy-start.42
  449.6 1.0 copy-start.13
  449.6 1.3 copy-start.14
  460.5 0.7 copy-start.37
  460.6 635.2 %reduce-scatter.20.cloned.1.call-start = ((), (), s32[]{:S(2)}) async-start(), calls=%async_computation.20 | async-start | bytes 2228224 | tf_op jit(solution)/shard_map/reduce_scatter | solution.py:279
  500.0 608.7 %reduce-scatter.30.cloned.1.call-start = ((), (), s32[]{:S(2)}) async-start(), calls=%async_computation.25 | async-start | bytes 294912 | tf_op jit(solution)/shard_map/reduce_scatter | solution.py:275
  500.2 8.6 copy-start.3
  522.1 695.0 %reduce-scatter.24.cloned.1.call-start = ((), (), s32[]{:S(2)}) async-start(), calls=%async_computation.22 | async-start | bytes 8912896 | tf_op jit(solution)/shard_map/reduce_scatter | solution.py:280
  691.5 633.2 %reduce-scatter.28.cloned.1.call-start = ((), (), s32[]{:S(2)}) async-start(), calls=%async_computation.24 | async-start | bytes 8912896 | tf_op jit(solution)/shard_map/reduce_scatter | solution.py:281
  882.9 530.9 %reduce-scatter.16.cloned.1.call-start = ((), (), s32[]{:S(2)}) async-start(), calls=%async_computation.18 | async-start | bytes 6684672 | tf_op jit(solution)/shard_map/reduce_scatter | solution.py:278
  1029.8 0.7 copy-start.46
  1029.8 1.2 copy-start.38
  1031.0 8.3 copy-start.39
  1031.0 8.3 copy-start.40
  1031.1 8.3 copy-start.43
  1031.1 8.3 copy-start.45
  1175.0 289.2 %copy-start.34 = (f32[12,32]{1,0:T(8,128)}, f32[12,32]{1,0:T(8,128)S(1)}, u32[]{:S(2)}) copy-start(f32[12,32]{1,0:T(8,128)S(1)} %get-tuple-element.63) | copy-start | bytes 4612
  1418.7 45.4 %copy-start.33 = (f32[12,32]{1,0:T(8,128)S(1)}, f32[12,32]{1,0:T(8,128)}, u32[]{:S(2)}) copy-start(f32[12,32]{1,0:T(8,128)} %param.20) | copy-start | bytes 4612
  1418.7 46.1 %copy-start.6 = (f32[256,512]{1,0:T(8,128)S(1)}, f32[256,512]{1,0:T(8,128)}, u32[]{:S(2)}) copy-start(f32[256,512]{1,0:T(8,128)} %param.19) | copy-start | bytes 1572868
  1418.7 46.1 %copy-start.10 = (f32[256,512]{1,0:T(8,128)S(1)}, f32[256,512]{1,0:T(8,128)}, u32[]{:S(2)}) copy-start(f32[256,512]{1,0:T(8,128)} %reduce-scatter.28.cloned.1.call-done) | copy-start | bytes 1572868
  1464.8 3.6 copy-start.8
  1464.8 3.6 copy-start.9
  1464.8 3.6 copy-start.18
  1468.4 2.3 copy-start.20
  1468.4 2.3 copy-start.21
  1468.5 2.3 copy-start.25
  1469.7 2.6 copy-start.11
  1469.7 2.6 copy-start.12
  1469.7 2.6 copy-start.19
Sparse Core Ops, SparseCore 0:
  17.2 63.0 all-gather.8
  82.5 40.1 all-gather.14
  124.8 31.7 all-gather.12
  158.6 33.0 all-gather.10
  193.7 74.2 all-gather.16
  270.1 72.8 all-gather.18
  345.3 97.8 reduce-scatter.11
  445.5 54.3 reduce-scatter.17
  502.2 189.2 reduce-scatter.21
  693.6 189.2 reduce-scatter.25
  885.2 144.5 reduce-scatter.13
  1033.9 61.7 reduce-scatter.19
  1098.6 9.9 reduce-scatter.29
  1113.1 103.9 reduce-scatter.23
  1221.6 103.0 reduce-scatter.27
  1329.0 84.6 reduce-scatter.15
where the time goes:
time: 1490 us; the launch traced here: 1480 us
  waiting for transfers between devices  1040 us (70%)
  matrix products  187 us (13%)
  blocking collectives  163 us (11%)
  other arithmetic  44.8 us (3%)
  local copies, waits for them, and re-layouts  28.9 us (2%)
  between operations  18.9 us (1%)
    reduce_scatter x1, waiting for transfers between devices, shards(): lax.psum_scatter(down_part, 'shard', scatter_dimension=1, tiled=True)  191 us
    reduce_scatter x1, waiting for transfers between devices, shards(): lax.psum_scatter(up_part, 'shard', scatter_dimension=1, tiled=True)  169 us
    reduce_scatter x1, waiting for transfers between devices, shards(): lax.psum_scatter(qkv_part, 'shard', scatter_dimension=1, tiled=True)  147 us
    reduce_scatter x1, waiting for transfers between devices, shards(): lax.psum_scatter(group_sums[3], 'dp', scatter_dimension=0, tiled=True)  106 us
    reduce_scatter x1, waiting for transfers between devices, shards(): lax.psum_scatter(group_sums[0], 'dp', scatter_dimension=0, tiled=True)  87.3 us
    unnamed x1, blocking collectives  65.1 us
    all_gather x1, waiting for transfers between devices, shards(): lax.all_gather(columns_full[3], 'dp', axis=0, tiled=True)  60.7 us
    reduce_scatter x1, waiting for transfers between devices, shards(): lax.psum_scatter(group_sums[1], 'dp', scatter_dimension=0, tiled=True)  53.7 us
  transfers between devices with their start and end apart: 16, of which 15 were waited for; matrix products, arithmetic and copies ran while one was open for 16% of the time, Pallas kernels for 0%

commit v1 on v0

--- a/solution.py
+++ b/solution.py
@@ -147,8 +147,11 @@
     cosine_table, sine_table = rotary_tables(positions, ROT)
     query_bf = rotate(query_raw, cosine_table, sine_table).astype(jnp.bfloat16)
     key_bf = rotate(key_raw, cosine_table, sine_table).astype(jnp.bfloat16).reshape(local_rows, D)
-    key_piece = lax.all_gather(key_bf, "shard", axis=0, tiled=True)
-    value_piece = lax.all_gather(value_bf, "shard", axis=0, tiled=True)
+    key_piece, value_piece = jnp.split(
+        lax.all_gather(jnp.concatenate([key_bf, value_bf], axis=1), "shard", axis=0, tiled=True),
+        [key_bf.shape[1]],
+        axis=1,
+    )
     piece_rows = key_piece.shape[0]
     key_heads = key_piece.reshape(piece_rows, head_count, HD)
     value_heads = value_piece.reshape(piece_rows, head_count, HD)

time: 1490 us -> 1550 us (1.040)
  waiting for transfers between devices: 1040 us -> 1060 us
  local copies, waits for them, and re-layouts: 28.9 us -> 45.3 us
    reduce_scatter x1, waiting for transfers between devices: 42.1 us -> 106 us  [shards(): lax.psum_scatter(group_sums[2], 'dp', scatter_dimension=0, tiled=True)]
    reduce_scatter x1, waiting for transfers between devices: 106 us -> 42.1 us  [shards(): lax.psum_scatter(group_sums[3], 'dp', scatter_dimension=0, tiled=True)]
    all_gather x2 -> x3, waiting for transfers between devices: 45.6 us -> 98.9 us  [the longest x1 42 us: shards(): lax.all_gather(jnp.concatenate([key_bf, value_bf], axis=1), 'shard', axis...]
    all_gather x1, waiting for transfers between devices: 60.7 us -> 25.2 us  [shards(): lax.all_gather(columns_full[3], 'dp', axis=0, tiled=True)]
    reduce_scatter x1, waiting for transfers between devices: 191 us -> 168 us  [shards(): lax.psum_scatter(down_part, 'shard', scatter_dimension=1, tiled=True)]
    reduce_scatter x1, waiting for transfers between devices: 169 us -> 191 us  [shards(): lax.psum_scatter(up_part, 'shard', scatter_dimension=1, tiled=True)]
    dot_general x1 -> x2, matrix products: 17.5 us -> 33.6 us  [shards(): jnp.einsum('qhd,khd->hqk', query_bf, key_heads, preferred_element_type=jn...]
  transfers between devices with their start and end apart: 16 -> 17, of which waited for: 15 -> 15; matrix products, arithmetic and copies ran while one was open for 16% -> 17% of each run, Pallas kernels for 0% -> 0%
where the time goes in v1:
time: 1550 us; the launch traced here: 1540 us
  waiting for transfers between devices  1060 us (68%)
  matrix products  202 us (13%)
  blocking collectives  163 us (11%)
  other arithmetic  46.5 us (3%)
  local copies, waits for them, and re-layouts  45.3 us (3%)
  between operations  19.2 us (1%)
    reduce_scatter x1, waiting for transfers between devices, shards(): lax.psum_scatter(up_part, 'shard', scatter_dimension=1, tiled=True)  191 us
    reduce_scatter x1, waiting for transfers between devices, shards(): lax.psum_scatter(down_part, 'shard', scatter_dimension=1, tiled=True)  168 us
    reduce_scatter x1, waiting for transfers between devices, shards(): lax.psum_scatter(qkv_part, 'shard', scatter_dimension=1, tiled=True)  147 us
    reduce_scatter x1, waiting for transfers between devices, shards(): lax.psum_scatter(group_sums[2], 'dp', scatter_dimension=0, tiled=True)  106 us
    reduce_scatter x1, waiting for transfers between devices, shards(): lax.psum_scatter(group_sums[0], 'dp', scatter_dimension=0, tiled=True)  87.3 us
    unnamed x1, blocking collectives  65.1 us
    reduce_scatter x1, waiting for transfers between devices, shards(): lax.psum_scatter(jnp.concatenate([key_terms, value_terms], axis=1), 'shar...  62.8 us
    reduce_scatter x1, waiting for transfers between devices, shards(): lax.psum_scatter(group_sums[1], 'dp', scatter_dimension=0, tiled=True)  53.9 us
  transfers between devices with their start and end apart: 17, of which 15 were waited for; matrix products, arithmetic and copies ran while one was open for 17% of the time, Pallas kernels for 0%

profile of v1, /device:TPU:0, one launch (start us, length us, event | category | flops | bytes accessed | tf_op | source)
XLA Modules:
  0.0 1538.2 jit_solution(15526165931220188069)
XLA Ops:
  8.4 8.6 all_gather.41
  18.0 5.0 all_gather.44
  23.2 4.4 all-gather
  27.6 22.3 %all-gather.1 = bf16[16,64,12]{1,2,0:T(8,128)(2,1)S(1)} all-gather(bf16[1,64,12]{1,2,0:T(8,128)(2,1)S(1)} %reshape.343), channel_id=1, replica_groups=mesh['dp'=16,'shard'=2] {'dp'}, dimensions={0}, use_global_device_ids=true | all-gather | bytes 26112 | tf_op jit(solution)/shard_map/all_gather | solution.py:129
  51.3 29.0 %all-gather.10.cloned.1.call-done = bf16[1024,3072]{1,0:T(8,128)(2,1)} async-done(((bf16[64,3072]{1,0:T(8,128)(2,1)}), bf16[1024,3072]{1,0:T(8,128)(2,1)}) %all-gather.10.cloned.1.call-update) | async-done | bytes 6291472 | tf_op jit(solution)/shard_map/all_gather | solution.py:125
  80.3 5.7 fusion.29
  86.1 2.3 slice_add_fusion
  90.1 2.9 copy.82
  93.0 1.8 copy.79
  96.3 2.0 subtract_convert_fusion.1
  99.5 1.6 copy.80
  103.7 9.4 all_gather.46
  113.2 8.4 all_gather.48
  123.9 3.3 convolution_convert_fusion
  128.7 1.7 slice.266
  130.4 26.3 %all-gather.22.cloned.1.call-done = bf16[1024,1024]{1,0:T(8,128)(2,1)} async-done(((bf16[512,1024]{1,0:T(8,128)(2,1)}), bf16[1024,1024]{1,0:T(8,128)(2,1)}) %all-gather.22.cloned.1.call-update) | async-done | bytes 2097168 | tf_op jit(solution)/shard_map/all_gather | solution.py:205
  156.7 4.0 copy.85
  160.7 30.5 %all-gather.20.cloned.1.call-done = bf16[1024,1024]{0,1:T(8,128)(2,1)} async-done(((bf16[512,1024]{0,1:T(8,128)(2,1)}), bf16[1024,1024]{0,1:T(8,128)(2,1)}) %all-gather.20.cloned.1.call-update) | async-done | bytes 2097168 | tf_op jit(solution)/shard_map/all_gather | solution.py:204
  191.2 16.7 %fusion.62 = f32[16,512,1024]{2,1,0:T(8,128)} fusion(bf16[1024,16,64]{0,2,1:T(8,128)(2,1)} %bitcast.171, bf16[512,16,48]{0,2,1:T(8,128)(2,1)S(1)} %slice.266, bf16[512,16,8]{0,2,1:T(8,128)(2,1)S(1)} %copy-done.14, bf16[512,16,8]{0,2,1:T(8,128)(2,1)S(1)} %get-tuple-element.75), kind=kOutput, calls=%fused_computation.163 | convolution fusion | flops 1076887552 | bytes 36700160 | tf_op jit(solution)/shard_map/qhd,khd->hqk/dot_general | solution.py:214
  207.9 42.0 %all-gather.12.cloned.1.call-done = bf16[1024,2048]{1,0:T(8,128)(2,1)} async-done(((bf16[512,2048]{1,0:T(8,128)(2,1)}), bf16[1024,2048]{1,0:T(8,128)(2,1)}) %all-gather.12.cloned.1.call-update) | async-done | bytes 4194320 | tf_op jit(solution)/shard_map/all_gather | solution.py:151
  249.9 4.0 fusion.64
  253.9 3.9 copy.83
  257.9 2.5 copy.81
  260.4 16.9 %fusion = (f32[16,512]{1,0:T(8,128)S(1)}, f32[16,512,1024]{2,1,0:T(8,128)}) fusion(pred[512,1024]{1,0:T(8,128)(4,1)} %fusion.19, bf16[1024,16,64]{0,2,1:T(8,128)(2,1)} %bitcast.184, bf16[512,16,48]{0,2,1:T(8,128)(2,1)S(1)} %slice.266, bf16[512,16,8]{0,2,1:T(8,128)(2,1)S(1)} %copy-done.14, bf16[512,16,8]{0,2,1:T(8,128)(2,1)S(1)} %get-tuple-element.75), kind=kOutput, calls=%fused_computation.3 | convolution fusion | flops 1102045184 | bytes 37257216 | tf_op jit(solution)/shard_map/qhd,khd->hqk/dot_general | solution.py:163
  277.3 16.6 %multiply_reduce_fusion.4 = (f32[512,16]{0,1:T(8,128)S(1)}, bf16[512,16,64]{0,2,1:T(8,128)(2,1)}) fusion(bf16[512,1024]{0,1:T(8,128)(2,1)} %copy.84, f32[512,16]{0,1:T(8,128)S(1)} %bitcast.195, bf16[1024,16,64]{0,2,1:T(8,128)(2,1)} %bitcast.183, f32[16,512,1024]{2,1,0:T(8,128)} %get-tuple-element.115, pred[512,1024]{1,0:T(8,128)(4,1)} %fusion.19), kind=kOutput, calls=%fused_computation.35 | convolution fusion | flops 1101520896 | bytes 38338560 | tf_op jit(solution)/shard_map/hqk,khd->qhd/dot_general | solution.py:167
  293.9 22.6 %multiply_convert_fusion = bf16[16,512,1024]{2,1,0:T(8,128)(2,1)} fusion(f32[16,512,1024]{2,1,0:T(8,128)} %fusion.62, f32[16,512]{1,0:T(8,128)S(1)} %bitcast.217, f32[16,512]{1,0:T(8,128)S(1)} %log.7, pred[512,1024]{1,0:T(8,128)(4,1)} %fusion.19, bf16[512,16,64]{0,2,1:T(8,128)(2,1)} %bitcast.189, bf16[1024,16,64]{0,2,1:T(8,128)(2,1)S(1)} %bitcast.182), kind=kOutput, calls=%fused_computation | convolution fusion | flops 1132462080 | bytes 54067200 | tf_op jit(solution)/shard_map/qhd,khd->hqk/dot_general | solution.py:218
  316.5 9.1 fusion.61
  325.7 17.1 %fusion.5 = f32[16,64,1024]{2,1,0:T(8,128)} fusion(bf16[512,16,64]{0,2,1:T(8,128)(2,1)} %bitcast.190, f32[16,512,1024]{2,1,0:T(8,128)} %fusion.62, f32[16,512]{1,0:T(8,128)} %copy-done.32, pred[512,1024]{1,0:T(8,128)(4,1)} %fusion.19), kind=kOutput, calls=%fused_computation.7 | convolution fusion | flops 1107296256 | bytes 39354368 | tf_op jit(solution)/shard_map/hqk,qhd->khd/dot_general | solution.py:232
  342.8 6.8 pad_maximum_fusion
  351.2 3.2 fusion.70
  356.0 9.9 multiply_convert_fusion.1
  365.9 2.0 copy-done.48
  367.8 8.3 fusion.71
  376.2 25.2 %all-gather.18.cloned.1.call-done = bf16[4096,1024]{1,0:T(8,128)(2,1)} async-done(((bf16[256,1024]{1,0:T(8,128)(2,1)}), bf16[4096,1024]{1,0:T(8,128)(2,1)}) %all-gather.18.cloned.1.call-update) | async-done | bytes 8388624 | tf_op jit(solution)/shard_map/all_gather | solution.py:128
  401.4 10.7 fusion.68
  412.1 2.1 copy-done.49
  414.2 8.4 fusion.15
  422.9 13.2 convolution_bitcast_fusion
  436.1 2.7 slice.189
  438.8 62.8 %reduce-scatter.12.cloned.1.call-done = f32[512,2048]{0,1:T(8,128)} async-done(((f32[1024,2048]{0,1:T(8,128)}), f32[512,2048]{0,1:T(8,128)}) %reduce-scatter.12.cloned.1.call-update) | async-done | bytes 4194320 | tf_op jit(solution)/shard_map/reduce_scatter | solution.py:238
  501.6 2.5 slice_reduce_fusion
  504.3 1.8 slice.264
  509.3 9.6 fusion.24
  519.8 38.5 %reduce-scatter.18.cloned.1.call-done = f32[1024,512]{1,0:T(8,128)} async-done(((f32[1024,1024]{1,0:T(8,128)}), f32[1024,512]{1,0:T(8,128)}) %reduce-scatter.18.cloned.1.call-update) | async-done | bytes 2097168 | tf_op jit(solution)/shard_map/reduce_scatter | solution.py:275
  558.6 8.5 fusion.25
  567.2 1.6 fusion.22
  569.0 11.7 multiply_reduce_fusion
  581.8 167.8 %reduce-scatter.26.cloned.1.call-done = f32[4096,512]{1,0:T(8,128)} async-done(((f32[4096,1024]{1,0:T(8,128)}), f32[4096,512]{1,0:T(8,128)}) %reduce-scatter.26.cloned.1.call-update) | async-done | bytes 8388624 | tf_op jit(solution)/shard_map/reduce_scatter | solution.py:277
  749.7 191.5 %reduce-scatter.22.cloned.1.call-done = f32[1024,2048]{1,0:T(8,128)} async-done(((f32[1024,4096]{1,0:T(8,128)}), f32[1024,2048]{1,0:T(8,128)}) %reduce-scatter.22.cloned.1.call-update) | async-done | bytes 8388624 | tf_op jit(solution)/shard_map/reduce_scatter | solution.py:276
  941.3 146.7 %reduce-scatter.14.cloned.1.call-done = f32[1024,1536]{1,0:T(8,128)} async-done(((f32[1024,3072]{1,0:T(8,128)}), f32[1024,1536]{1,0:T(8,128)}) %reduce-scatter.14.cloned.1.call-update) | async-done | bytes 6291472 | tf_op jit(solution)/shard_map/reduce_scatter | solution.py:274
  1089.2 8.3 fusion.69
  1097.6 2.6 add_add_fusion
  1100.2 53.9 %reduce-scatter.20.cloned.1.call-done = f32[64,512]{1,0:T(8,128)} async-done(((f32[1024,512]{1,0:T(8,128)}), f32[64,512]{1,0:T(8,128)}) %reduce-scatter.20.cloned.1.call-update) | async-done | bytes 131088 | tf_op jit(solution)/shard_map/reduce_scatter | solution.py:282
  1154.1 1.5 multiply_reduce_fusion.11
  1155.6 11.1 reduce-scatter.30.cloned.1.call-done
  1166.8 65.1 %all-reduce = f32[12,16,1,32]{3,2,1,0:T(1,128)S(1)} all-reduce(f32[12,16,1,32]{3,2,1,0:T(1,128)} %bitcast.193), channel_id=12, replica_groups=mesh['dp'=16,'shard'=2] {'dp'}, use_global_device_ids=true, to_apply=%region_28.29.clone | all-reduce | flops 6144 | bytes 49152
  1233.1 42.1 %reduce-scatter.28.cloned.1.call-done = f32[256,512]{1,0:T(8,128)} async-done(((f32[4096,512]{1,0:T(8,128)}), f32[256,512]{1,0:T(8,128)}) %reduce-scatter.28.cloned.1.call-update) | async-done | bytes 524304 | tf_op jit(solution)/shard_map/reduce_scatter | solution.py:284
  1275.2 1.8 multiply_reduce_fusion.8
  1277.0 105.8 %reduce-scatter.24.cloned.1.call-done = f32[64,2048]{1,0:T(8,128)} async-done(((f32[1024,2048]{1,0:T(8,128)}), f32[64,2048]{1,0:T(8,128)}) %reduce-scatter.24.cloned.1.call-update) | async-done | bytes 524304 | tf_op jit(solution)/shard_map/reduce_scatter | solution.py:283
  1382.8 1.8 multiply_reduce_fusion.9
  1384.6 87.3 %reduce-scatter.16.cloned.1.call-done = f32[64,1536]{1,0:T(8,128)} async-done(((f32[1024,1536]{1,0:T(8,128)}), f32[64,1536]{1,0:T(8,128)}) %reduce-scatter.16.cloned.1.call-update) | async-done | bytes 393232 | tf_op jit(solution)/shard_map/reduce_scatter | solution.py:281
  1471.9 1.7 multiply_reduce_fusion.10
  1476.9 4.5 multiply_add_fusion
  1481.4 39.6 %psum.7 = f32[]{:T(128)} all-reduce(f32[]{:T(128)S(6)} %add.283), channel_id=1, replica_groups=mesh['dp'=16,'shard'=2] {'dp','shard'}, use_global_device_ids=true, to_apply=%region_34.35 | all-reduce | flops 1 | bytes 8 | tf_op jit(solution)/shard_map/psum | solution.py:299
  (210 shorter events, 35.7 us)
Async XLA Ops:
  7.2 16.0 %copy-start.33 = (f32[12,32]{1,0:T(8,128)S(1)}, f32[12,32]{1,0:T(8,128)}, u32[]{:S(2)}) copy-start(f32[12,32]{1,0:T(8,128)} %param.20) | copy-start | bytes 4612
  7.2 42.8 %copy-start = (f32[512,1024]{1,0:T(8,128)S(1)}, f32[512,1024]{1,0:T(8,128)}, u32[]{:S(2)}) copy-start(f32[512,1024]{1,0:T(8,128)} %param.13) | copy-start | bytes 6291460
  7.2 73.1 %all-gather.10.cloned.1.call-start = ((), (), s32[]{:S(2)}) async-start(), calls=%async_computation.10 | async-start | bytes 6684672 | tf_op jit(solution)/shard_map/all_gather | solution.py:125
  17.1 106.8 %all-gather.14.cloned.1.call-start = ((), (), s32[]{:S(2)}) async-start(), calls=%async_computation.12 | async-start | bytes 2228224 | tf_op jit(solution)/shard_map/all_gather | solution.py:126
  23.1 133.6 %all-gather.22.cloned.1.call-start = ((), (), s32[]{:S(2)}) async-start(), calls=%async_computation.16 | async-start | bytes 3145728 | tf_op jit(solution)/shard_map/all_gather | solution.py:205
  51.3 34.8 %copy-start.36 = (f32[1,1024]{1,0:T(1,128)}, f32[1,1024]{1,0:T(1,128)S(1)}, u32[]{:S(2)}) copy-start(f32[1,1024]{1,0:T(1,128)S(1)} %get-tuple-element.102) | copy-start | bytes 12292
  51.3 34.8 %copy-start.42 = (f32[1,1024]{1,0:T(1,128)}, f32[1,1024]{1,0:T(1,128)S(1)}, u32[]{:S(2)}) copy-start(f32[1,1024]{1,0:T(1,128)S(1)} %get-tuple-element.101) | copy-start | bytes 12292
  86.1 2.4 copy-start.31
  88.4 102.8 %all-gather.20.cloned.1.call-start = ((), (), s32[]{:S(2)}) async-start(), calls=%async_computation.15 | async-start | bytes 3145728 | tf_op jit(solution)/shard_map/all_gather | solution.py:204
  90.1 6.2 copy-start.28
  99.4 1.6 copy-start.3
  99.4 150.5 %all-gather.12.cloned.1.call-start = ((), (), s32[]{:S(2)}) async-start(), calls=%async_computation.11 | async-start | bytes 6291456 | tf_op jit(solution)/shard_map/all_gather | solution.py:151
  102.6 1.0 copy-start.8
  102.6 10.5 copy-start.6
  102.6 252.8 %all-gather.16.cloned.1.call-start = ((), (), s32[]{:S(2)}) async-start(), calls=%async_computation.13 | async-start | bytes 8912896 | tf_op jit(solution)/shard_map/all_gather | solution.py:127
  103.6 19.4 %copy-start.4 = (f32[512,1024]{1,0:T(8,128)S(1)}, f32[512,1024]{1,0:T(8,128)}, u32[]{:S(2)}) copy-start(f32[512,1024]{1,0:T(8,128)} %param.14) | copy-start | bytes 6291460
  113.1 288.3 %all-gather.18.cloned.1.call-start = ((), (), s32[]{:S(2)}) async-start(), calls=%async_computation.14 | async-start | bytes 8912896 | tf_op jit(solution)/shard_map/all_gather | solution.py:128
  121.6 380.0 %reduce-scatter.12.cloned.1.call-start = ((), (), s32[]{:S(2)}) async-start(), calls=%async_computation.17 | async-start | bytes 12582912 | tf_op jit(solution)/shard_map/reduce_scatter | solution.py:238
  123.9 3.3 copy-start.18
  130.3 60.9 %copy-start.14 = (bf16[512,16,8]{0,2,1:T(8,128)(2,1)S(1)}, bf16[512,16,8]{0,2,1:T(8,128)(2,1)}, u32[]{:S(2)}) copy-start(bf16[512,16,8]{0,2,1:T(8,128)(2,1)} %get-tuple-element.76) | copy-start | bytes 393220
  277.3 16.6 %copy-start.32 = (f32[16,512]{1,0:T(8,128)}, f32[16,512]{1,0:T(8,128)S(1)}, u32[]{:S(2)}) copy-start(f32[16,512]{1,0:T(8,128)S(1)} %log.7) | copy-start | bytes 98308
  277.3 16.6 %copy-start.5 = (bf16[1024,1024]{0,1:T(8,128)(2,1)S(1)}, bf16[1024,1024]{0,1:T(8,128)(2,1)}, u32[]{:S(2)}) copy-start(bf16[1024,1024]{0,1:T(8,128)(2,1)} %copy.85) | copy-start | bytes 6291460
  293.9 22.6 %copy-start.15 = (bf16[512,16,8]{0,2,1:T(8,128)(2,1)S(1)}, bf16[512,16,8]{0,2,1:T(8,128)(2,1)}, u32[]{:S(2)}) copy-start(bf16[512,16,8]{0,2,1:T(8,128)(2,1)} %get-tuple-element.76) | copy-start | bytes 393220
  349.6 1.2 copy-start.19
  349.6 1.6 copy-start.45
  349.6 208.7 %reduce-scatter.18.cloned.1.call-start = ((), (), s32[]{:S(2)}) async-start(), calls=%async_computation.20 | async-start | bytes 6291456 | tf_op jit(solution)/shard_map/reduce_scatter | solution.py:275
  354.4 1.6 copy-start.1
  354.4 395.3 %reduce-scatter.26.cloned.1.call-start = ((), (), s32[]{:S(2)}) async-start(), calls=%async_computation.24 | async-start | bytes 25165824 | tf_op jit(solution)/shard_map/reduce_scatter | solution.py:277
  365.9 2.0 copy-start.48
  376.1 565.1 %reduce-scatter.22.cloned.1.call-start = ((), (), s32[]{:S(2)}) async-start(), calls=%async_computation.22 | async-start | bytes 25165824 | tf_op jit(solution)/shard_map/reduce_scatter | solution.py:276
  412.1 2.1 copy-start.49
  422.6 665.3 %reduce-scatter.14.cloned.1.call-start = ((), (), s32[]{:S(2)}) async-start(), calls=%async_computation.18 | async-start | bytes 18874368 | tf_op jit(solution)/shard_map/reduce_scatter | solution.py:274
  504.1 2.0 copy-start.29
  504.1 2.0 copy-start.30
  504.3 3.4 copy-start.2
  506.1 1.9 copy-start.20
  507.7 1.6 copy-start.37
  507.7 1.6 copy-start.43
  508.0 1.0 copy-start.16
  508.0 1.3 copy-start.17
  518.9 635.2 %reduce-scatter.20.cloned.1.call-start = ((), (), s32[]{:S(2)}) async-start(), calls=%async_computation.21 | async-start | bytes 2228224 | tf_op jit(solution)/shard_map/reduce_scatter | solution.py:282
  558.3 608.4 %reduce-scatter.30.cloned.1.call-start = ((), (), s32[]{:S(2)}) async-start(), calls=%async_computation.26 | async-start | bytes 294912 | tf_op jit(solution)/shard_map/reduce_scatter | solution.py:278
  581.8 693.4 %reduce-scatter.28.cloned.1.call-start = ((), (), s32[]{:S(2)}) async-start(), calls=%async_computation.25 | async-start | bytes 8912896 | tf_op jit(solution)/shard_map/reduce_scatter | solution.py:284
  749.7 633.1 %reduce-scatter.24.cloned.1.call-start = ((), (), s32[]{:S(2)}) async-start(), calls=%async_computation.23 | async-start | bytes 8912896 | tf_op jit(solution)/shard_map/reduce_scatter | solution.py:283
  941.2 530.7 %reduce-scatter.16.cloned.1.call-start = ((), (), s32[]{:S(2)}) async-start(), calls=%async_computation.19 | async-start | bytes 6684672 | tf_op jit(solution)/shard_map/reduce_scatter | solution.py:281
  1087.9 1.2 copy-start.39
  1089.2 8.3 copy-start.40
  1089.2 8.3 copy-start.41
  1089.2 8.3 copy-start.44
  1089.2 8.3 copy-start.46
  1233.1 288.6 %copy-start.35 = (f32[12,32]{1,0:T(8,128)}, f32[12,32]{1,0:T(8,128)S(1)}, u32[]{:S(2)}) copy-start(f32[12,32]{1,0:T(8,128)S(1)} %get-tuple-element.63) | copy-start | bytes 4612
  1476.9 44.9 %copy-start.34 = (f32[12,32]{1,0:T(8,128)S(1)}, f32[12,32]{1,0:T(8,128)}, u32[]{:S(2)}) copy-start(f32[12,32]{1,0:T(8,128)} %param.20) | copy-start | bytes 4612
  1476.9 46.1 %copy-start.24 = (f32[64,512]{1,0:T(8,128)S(1)}, f32[64,512]{1,0:T(8,128)}, u32[]{:S(2)}) copy-start(f32[64,512]{1,0:T(8,128)} %param.17) | copy-start | bytes 393220
  1476.9 46.1 %copy-start.25 = (f32[64,512]{1,0:T(8,128)S(1)}, f32[64,512]{1,0:T(8,128)}, u32[]{:S(2)}) copy-start(f32[64,512]{1,0:T(8,128)} %reduce-scatter.20.cloned.1.call-done) | copy-start | bytes 393220
  1476.9 46.1 %copy-start.26 = (f32[2,64,512]{2,1,0:T(8,128)S(1)}, f32[2,64,512]{2,1,0:T(8,128)}, u32[]{:S(2)}) copy-start(f32[2,64,512]{2,1,0:T(8,128)} %param.22) | copy-start | bytes 786436
  1476.9 47.6 %copy-start.12 = (f32[64,1536]{1,0:T(8,128)S(1)}, f32[64,1536]{1,0:T(8,128)}, u32[]{:S(2)}) copy-start(f32[64,1536]{1,0:T(8,128)} %param.16) | copy-start | bytes 1179652
  1476.9 47.6 %copy-start.13 = (f32[64,1536]{1,0:T(8,128)S(1)}, f32[64,1536]{1,0:T(8,128)}, u32[]{:S(2)}) copy-start(f32[64,1536]{1,0:T(8,128)} %reduce-scatter.16.cloned.1.call-done) | copy-start | bytes 1179652
  1481.4 43.1 %copy-start.23 = (f32[2,64,1536]{2,1,0:T(8,128)S(1)}, f32[2,64,1536]{2,1,0:T(8,128)}, u32[]{:S(2)}) copy-start(f32[2,64,1536]{2,1,0:T(8,128)} %param.21) | copy-start | bytes 2359300
  1524.5 2.1 copy-start.7
  1524.5 2.1 copy-start.10
  1524.5 2.0 copy-start.21
  1526.6 2.3 copy-start.9
  1526.6 2.3 copy-start.11
  1526.6 2.3 copy-start.22
  (3 other events, 2.0 us)
Sparse Core Ops, SparseCore 0:
  17.2 63.0 all-gather.9
  82.5 40.2 all-gather.13
  124.9 31.7 all-gather.21
  158.1 33.0 all-gather.19
  193.2 56.7 all-gather.11
  252.0 74.2 all-gather.15
  328.4 72.8 all-gather.17
  403.6 97.8 reduce-scatter.11
  503.9 54.3 reduce-scatter.17
  560.4 189.1 reduce-scatter.25
  752.0 189.1 reduce-scatter.21
  943.4 144.5 reduce-scatter.13
  1092.2 61.7 reduce-scatter.19
  1156.7 9.9 reduce-scatter.29
  1171.2 103.9 reduce-scatter.27
  1279.7 103.0 reduce-scatter.23
  1387.2 84.7 reduce-scatter.15
